TPU v7x, 512 devices: a whole 4x4x16 slice. The times are simulated.
512 devices in a mesh: probe: 16 (over y, x), space: 32 (over z, core).
Axes of the slice: x: 4, y: 4, z: 16, core: 2. Of those that a mesh axis runs over, the one named last changes fastest.
Arguments:
- probes: float32 [128, 131072], P('probe', 'space'), may hold values from -6 to 6
- sensitivity: float32 [8, 8, 65536], P(None, None, 'space'), may hold values from -2.1 to 2.1
- obs_weight: float32 [8, 65536], P(None, 'space'), may hold values from 0.5 to 4
- prior_weight: float32 [131072], P('space'), may hold values from 0.2 to 2
- connectivity: int32 [8, 65536], P(None, 'space'), may hold values from 0 to 4351, as said below
Outputs:
- basis: float32 [128, 131072], P('probe', 'space')
- factor: float32 [128, 128], replicated
Inputs may be any that keep to these rules, and one draw needn't show every extreme that they name: Each column holds 8 distinct numbers. For an element of the block of device d of space (columns d * 2048 to (d + 1) * 2048 - 1), connectivity + d * 4096 - 128 is an existing node, and the values 0 and 4351 are both named wherever those nodes exist.
All inputs are finite; a program needn't handle non-finite values.
Results may differ from a plain program's by a relative error of at most 0.0003.
Values sent between devices are 32-bit elements; how exact they have to be, the bound alone decides.
No kernel may reach another device: no remote copies, remote signals or barrier semaphores. Data moves between devices by JAX's collectives and lax.ppermute only.
A program may use at most 64 MiB of HBM per device.

v0:
```python
import math
import jax
import jax.numpy as jnp
from jax import lax
from jax.sharding import PartitionSpec as P

HALO = 128
highest = lax.Precision.HIGHEST


def extended_2(block, sides, width):
    for axis, dim in sides:
        count = lax.axis_size(axis)
        forward = [(i, i + 1) for i in range(count - 1)]
        backward = [(target, source) for source, target in forward]
        low = lax.ppermute(
            lax.slice_in_dim(block, block.shape[dim] - width, None, axis=dim), axis, forward
        )
        high = lax.ppermute(lax.slice_in_dim(block, 0, width, axis=dim), axis, backward)
        block = jnp.concatenate([low, block, high], axis=dim)
    return block


def shifted(block, axis, distance):
    devices = range(lax.axis_size(axis))
    route = [(i - distance, i) for i in devices if i - distance in devices]
    return lax.ppermute(block, axis, route)


def element_images(extended, sensitivity, obs_weight, local):
    gathered = extended[:, local]
    gauss_count = sensitivity.shape[0]
    corner_count = sensitivity.shape[1]
    observed = []
    for gauss in range(gauss_count):
        total = gathered[:, 0, :] * sensitivity[gauss, 0][None, :]
        for corner in range(1, corner_count):
            total = total + gathered[:, corner, :] * sensitivity[gauss, corner][None, :]
        observed.append(total * obs_weight[gauss][None, :])
    pulled = []
    for corner in range(corner_count):
        total = observed[0] * sensitivity[0, corner][None, :]
        for gauss in range(1, gauss_count):
            total = total + observed[gauss] * sensitivity[gauss, corner][None, :]
        pulled.append(total)
    pulled = jnp.stack(pulled, axis=1)
    return jnp.zeros(extended.shape, jnp.float32).at[:, local].add(pulled)


def gram_over_space(partial_value):
    return lax.psum(partial_value, "space")


def orthonormal(rows, reduce_gram):
    gram_first = reduce_gram(
        jnp.dot(rows, rows.T, precision=highest, preferred_element_type=jnp.float32)
    )
    lower_first = jnp.linalg.cholesky(gram_first)
    basis_first = lax.linalg.triangular_solve(lower_first, rows, left_side=True, lower=True)
    gram_second = reduce_gram(
        jnp.dot(basis_first, basis_first.T, precision=highest, preferred_element_type=jnp.float32)
    )
    lower_second = jnp.linalg.cholesky(gram_second)
    basis = lax.linalg.triangular_solve(lower_second, basis_first, left_side=True, lower=True)
    factor = jnp.dot(
        lower_first, lower_second, precision=highest, preferred_element_type=jnp.float32
    ).T
    return (basis, factor)


def on_device(probes, sensitivity, obs_weight, prior_weight, connectivity):
    node_count = probes.shape[1]
    probe_count = probes.shape[0]
    extended = extended_2(probes, (("space", 1),), HALO)
    summed = element_images(extended, sensitivity, obs_weight, connectivity)
    lower_rim = shifted(summed[:, :HALO], "space", -1)
    upper_rim = shifted(summed[:, HALO + node_count :], "space", 1)
    images = summed[:, HALO : HALO + node_count] + prior_weight[None, :] * probes
    images = images.at[:, node_count - HALO :].add(lower_rim)
    images = images.at[:, :HALO].add(upper_rim)
    scale = math.sqrt(float(node_count * lax.axis_size("space")))
    whole = lax.all_gather(images, "probe", axis=0, tiled=True)
    basis, factor = orthonormal(whole, gram_over_space)
    basis = lax.dynamic_slice_in_dim(basis, lax.axis_index("probe") * probe_count, probe_count, 0)
    return (basis * scale, factor / scale)


def solution(mesh):
    return jax.shard_map(
        on_device,
        mesh=mesh,
        in_specs=(
            P("probe", "space"),
            P(None, None, "space"),
            P(None, "space"),
            P("space"),
            P(None, "space"),
        ),
        out_specs=(P("probe", "space"), P()),
        check_vma=False,
    )
```

profile of v0, /device:TPU:1, one launch (start us, length us, event | category | flops | bytes accessed | tf_op | source)
XLA Modules:
  0.0 697.5 jit_solution(16327532529719816883)
XLA Ops:
  7.2 0.7 fusion.30
  7.9 4.9 collective-permute-start
  12.8 5.1 collective-permute-start.1
  18.0 1.7 fusion.28
  19.7 1.7 fusion.27
  21.4 1.9 fusion.26
  23.3 1.3 fusion.31
  24.5 0.9 fusion.2
  25.4 1.2 fusion.29
  26.6 0.6 compare_reduce_fusion.2
  27.2 0.9 pad_maximum_fusion
  28.2 0.6 copy.43
  28.8 54.8 %gather_fusion = f32[16384,8]{1,0:T(8,128)} fusion(f32[8,4352]{0,1:T(8,128)S(1)} %copy.43, s32[16384]{0:T(1024)S(1)} %broadcast_clamp_fusion), kind=kCustom, calls=%fused_computation | custom fusion | bytes 1114112 | tf_op jit(solution)/shard_map/gather | solution.py:31
  83.6 5.5 copy.44
  89.1 0.6 multiply_add_fusion.1
  89.7 0.1 multiply_add_fusion.2
  89.8 0.1 multiply_add_fusion.3
  89.9 0.1 multiply_add_fusion.4
  90.0 0.1 multiply_add_fusion.5
  90.0 0.1 multiply_add_fusion.6
  90.1 0.1 multiply_add_fusion.7
  90.2 0.1 multiply_add_fusion.8
  90.2 0.1 copy.51
  90.3 0.1 copy.50
  90.4 0.1 copy.49
  90.5 0.1 copy.48
  90.6 0.1 copy.47
  90.6 0.1 copy.46
  90.7 0.1 copy.45
  90.8 0.1 copy.52
  90.9 0.8 stack.2
  91.7 4.6 copy.63
  96.3 88.2 %scatter_custom_fusion = f32[8,4352]{0,1:T(8,128)S(1)} fusion(s32[16384]{0:T(1024)S(1)} %bitcast.108, f32[16384,8]{1,0:T(8,128)} %bitcast.104, f32[]{:T(128)} %constant.95.clone.1), kind=kCustom, calls=%fused_computation.3 | custom fusion | flops 131072 | bytes 139776 | tf_op jit(solution)/shard_map/scatter-add | solution.py:47
  184.4 1.5 slice.540
  185.9 2.2 copy.64
  188.1 0.1 copy.65
  188.2 1.9 collective-permute-start.2
  190.2 3.7 collective-permute-start.3
  193.9 0.7 collective-permute-done.3
  194.6 0.6 fusion.21
  195.2 0.6 copy-done.1
  195.9 0.0 all-reduce.3.cloned.1.call-start
  195.9 62.5 %all-gather.2.cloned.1.call-done = f32[128,4096]{1,0:T(8,128)} async-done(((f32[8,4096]{1,0:T(8,128)}), f32[128,4096]{1,0:T(8,128)}) %all-gather.2.cloned.1.call-update) | async-done | bytes 2097168 | tf_op jit(solution)/shard_map/all_gather | solution.py:82
  258.5 4.7 fusion.32
  263.2 0.2 all-reduce.5.cloned.1.call-start
  263.4 187.4 %all-reduce.3.cloned.1.call-done = f32[128,128]{0,1:T(8,128)} async-done(((f32[128,128]{0,1:T(8,128)}), f32[128,128]{0,1:T(8,128)}) %all-reduce.3.cloned.1.call-update) | async-done | bytes 65552 | tf_op jit(solution)/shard_map/psum | solution.py:51
  450.9 0.9 copy.58
  451.8 0.9 fusion.8
  452.6 11.7 %cholesky.44 = f32[128,128]{1,0:T(8,128)S(1)} custom-call(f32[128,128]{1,0:T(8,128)S(1)} %fusion.8), custom_call_target="Cholesky" | custom-call | tf_op jit(solution)/shard_map/jit(cholesky)/cholesky | solution.py:58
  464.4 0.6 compare_reduce_fusion.1
  465.0 0.7 fusion.12
  465.7 9.8 %custom-call.6 = f32[1,128,128]{1,2,0:T(8,128)S(1)} custom-call(f32[1,128,128]{2,1,0:T(8,128)S(1)} %fusion.12), custom_call_target="InvertDiagBlocksLowerTriangular" | custom-call | tf_op jit(solution)/shard_map/triangular_solve/custom-call.0 | solution.py:59
  475.5 3.5 fusion.6
  479.0 2.4 fusion.33
  481.5 179.9 %all-reduce.5.cloned.1.call-done = f32[128,128]{0,1:T(8,128)} async-done(((f32[128,128]{0,1:T(8,128)}), f32[128,128]{0,1:T(8,128)}) %all-reduce.5.cloned.1.call-update) | async-done | bytes 65552 | tf_op jit(solution)/shard_map/psum | solution.py:51
  661.4 0.9 copy.60
  662.3 0.9 fusion.5
  663.2 11.9 %cholesky.55 = f32[128,128]{1,0:T(8,128)S(1)} custom-call(f32[128,128]{1,0:T(8,128)S(1)} %fusion.5), custom_call_target="Cholesky" | custom-call | tf_op jit(solution)/shard_map/jit(cholesky)/cholesky | solution.py:63
  675.2 0.6 compare_reduce_fusion
  675.8 2.1 convolution_multiply_fusion
  677.9 0.6 select_bitcast_fusion
  678.5 9.8 %custom-call.7 = f32[1,128,128]{1,2,0:T(8,128)S(1)} custom-call(f32[1,128,128]{2,1,0:T(8,128)S(1)} %select_bitcast_fusion), custom_call_target="InvertDiagBlocksLowerTriangular" | custom-call | tf_op jit(solution)/shard_map/triangular_solve/custom-call.0 | solution.py:64
  688.3 1.9 fusion.3
  690.2 0.7 dynamic-slice_multiply_fusion
  (20 shorter events, 0.3 us)
Async XLA Ops:
  7.2 251.3 %all-gather.2.cloned.1.call-start = ((), (), s32[]{:S(2)}) async-start(), calls=%async_computation | async-start | bytes 2228224 | tf_op jit(solution)/shard_map/all_gather | solution.py:82
  7.9 19.3 %collective-permute-start = (f32[8,128]{1,0:T(8,128)S(1)}, f32[8,128]{1,0:T(8,128)S(1)}, u32[]{:S(2)}, u32[]{:S(2)}) collective-permute-start(f32[8,128]{1,0:T(8,128)S(1)} %get-tuple-element.103), channel_id=1, source_target_pairs={{0,1},{1,2},{2,3},{3,4},{4,5},{5,6},{6,7},{7,8},{8,9},{9,10},{10,1... | collective-permute-start | bytes 12296 | tf_op jit(solution)/shard_map/ppermute | solution.py:16
  12.8 14.4 %collective-permute-start.1 = (f32[8,128]{1,0:T(8,128)S(1)}, f32[8,128]{1,0:T(8,128)S(1)}, u32[]{:S(2)}, u32[]{:S(2)}) collective-permute-start(f32[8,128]{1,0:T(8,128)S(1)} %get-tuple-element.104), channel_id=1, source_target_pairs={{1,0},{2,1},{3,2},{4,3},{5,4},{6,5},{7,6},{8,7},{9,8},{10,9},{11,1... | collective-permute-start | bytes 12296 | tf_op jit(solution)/shard_map/ppermute | solution.py:19
  185.9 7.9 %copy-start = (f32[8,4096]{1,0:T(8,128)S(1)}, f32[8,4096]{1,0:T(8,128)}, u32[]{:S(2)}) copy-start(f32[8,4096]{1,0:T(8,128)} %param.12) | copy-start | bytes 393220
  185.9 7.9 %copy-start.2 = (f32[4096]{0:T(1024)S(1)}, f32[4096]{0:T(1024)}, u32[]{:S(2)}) copy-start(f32[4096]{0:T(1024)} %param.15) | copy-start | bytes 49156
  188.2 5.7 collective-permute-start.2
  190.2 4.4 collective-permute-start.3
  195.2 0.7 copy-start.1
  195.9 255.0 %all-reduce.3.cloned.1.call-start = ((), (), s32[]{:S(2)}) async-start(), calls=%async_computation.1 | async-start | bytes 131072 | tf_op jit(solution)/shard_map/psum | solution.py:51
  263.2 398.2 %all-reduce.5.cloned.1.call-start = ((), (), s32[]{:S(2)}) async-start(), calls=%async_computation.2 | async-start | bytes 131072 | tf_op jit(solution)/shard_map/psum | solution.py:51
Sparse Core Ops, SparseCore 0:
  196.0 62.4 all-gather.1
  263.3 187.4 all-reduce.2
  481.6 179.7 all-reduce.4
where the time goes:
time: 698 us; the launch traced here: 697 us
  waiting for transfers between devices  431 us (62%)
  other arithmetic  141 us (20%)
  local copies, waits for them, and re-layouts  81.6 us (12%)
  starting transfers between devices  15.9 us (2%)
  matrix products  14.7 us (2%)
  between operations  14.1 us (2%)
    psum x2, waiting for transfers between devices, gram_over_space(): return lax.psum(partial_value, 'space')  367 us
    scatter-add x1, other arithmetic, element_images(): return jnp.zeros(extended.shape, jnp.float32).at[:, local].add(pulled)  88.2 us
    all_gather x1, waiting for transfers between devices, on_device(): whole = lax.all_gather(images, 'probe', axis=0, tiled=True)  62.5 us
    gather x2, local copies, waits for them, and re-layouts, element_images(): gathered = extended[:, local]  60.3 us
  transfers between devices with their start and end apart: 7, of which 4 were waited for; matrix products, arithmetic and copies ran while one was open for 1% of the time, Pallas kernels for 0%

commit v1 on v0

--- a/solution.py
+++ b/solution.py
@@ -79,7 +79,9 @@
     images = images.at[:, node_count - HALO :].add(lower_rim)
     images = images.at[:, :HALO].add(upper_rim)
     scale = math.sqrt(float(node_count * lax.axis_size("space")))
-    whole = lax.all_gather(images, "probe", axis=0, tiled=True)
+    whole = jnp.concatenate(
+        lax.all_to_all(jnp.stack([images] * lax.axis_size("probe")), "probe", 0, 0), axis=0
+    )
     basis, factor = orthonormal(whole, gram_over_space)
     basis = lax.dynamic_slice_in_dim(basis, lax.axis_index("probe") * probe_count, probe_count, 0)
     return (basis * scale, factor / scale)

time: 698 us -> 667 us (0.956)
  waiting for transfers between devices: 431 us -> 368 us
  blocking collectives: 0 us -> 31.7 us
    all_gather x1 -> x0, waiting for transfers between devices: 62.5 us -> none  [on_device(): whole = lax.all_gather(images, 'probe', axis=0, tiled=True)]
    all_to_all x0 -> x1, blocking collectives: none -> 31.7 us  [on_device(): lax.all_to_all(jnp.stack([images] * lax.axis_size('probe')), 'probe', 0, 0)]
  transfers between devices with their start and end apart: 7 -> 6, of which waited for: 4 -> 3; matrix products, arithmetic and copies ran while one was open for 1% -> 1% of each run, Pallas kernels for 0% -> 0%
where the time goes in v1:
time: 667 us; the launch traced here: 666 us
  waiting for transfers between devices  368 us (55%)
  other arithmetic  141 us (21%)
  local copies, waits for them, and re-layouts  82.2 us (12%)
  blocking collectives  31.7 us (5%)
  starting transfers between devices  15.9 us (2%)
  between operations  14.4 us (2%)
  matrix products  12.5 us (2%)
    psum x2, waiting for transfers between devices, gram_over_space(): return lax.psum(partial_value, 'space')  367 us
    scatter-add x1, other arithmetic, element_images(): return jnp.zeros(extended.shape, jnp.float32).at[:, local].add(pulled)  88.2 us
    gather x2, local copies, waits for them, and re-layouts, element_images(): gathered = extended[:, local]  60 us
    all_to_all x1, blocking collectives, on_device(): lax.all_to_all(jnp.stack([images] * lax.axis_size('probe')), 'probe', 0, 0)  31.7 us
  transfers between devices with their start and end apart: 6, of which 3 were waited for; matrix products, arithmetic and copies ran while one was open for 1% of the time, Pallas kernels for 0%

profile of v1, /device:TPU:1, one launch (start us, length us, event | category | flops | bytes accessed | tf_op | source)
XLA Modules:
  0.0 665.6 jit_solution(11118709685910277258)
XLA Ops:
  7.2 0.7 fusion.33
  7.9 4.9 collective-permute-start
  12.8 5.1 collective-permute-start.1
  18.0 1.7 fusion.31
  19.7 1.7 fusion.30
  21.4 1.9 fusion.29
  23.3 1.3 fusion.34
  24.5 0.9 fusion.6
  25.4 1.2 fusion.32
  26.6 0.6 compare_reduce_fusion.2
  27.2 0.9 pad_maximum_fusion
  28.2 0.6 copy.44
  28.8 54.4 %gather_fusion = f32[16384,8]{1,0:T(8,128)} fusion(f32[8,4352]{0,1:T(8,128)S(1)} %copy.44, s32[16384]{0:T(1024)S(1)} %broadcast_clamp_fusion), kind=kCustom, calls=%fused_computation | custom fusion | bytes 1114112 | tf_op jit(solution)/shard_map/gather | solution.py:31
  83.2 5.5 copy.45
  88.8 0.6 multiply_add_fusion.1
  89.4 0.1 multiply_add_fusion.2
  89.5 0.1 multiply_add_fusion.3
  89.6 0.1 multiply_add_fusion.4
  89.6 0.1 multiply_add_fusion.5
  89.7 0.1 multiply_add_fusion.6
  89.8 0.1 multiply_add_fusion.7
  89.8 0.1 multiply_add_fusion.8
  89.9 0.1 copy.52
  90.0 0.1 copy.51
  90.1 0.1 copy.50
  90.1 0.1 copy.49
  90.2 0.1 copy.48
  90.3 0.1 copy.47
  90.4 0.1 copy.46
  90.5 0.1 copy.53
  90.5 0.8 stack.4
  91.4 4.5 copy.64
  95.9 88.2 %scatter_custom_fusion = f32[8,4352]{0,1:T(8,128)S(1)} fusion(s32[16384]{0:T(1024)S(1)} %bitcast.110, f32[16384,8]{1,0:T(8,128)} %bitcast.106, f32[]{:T(128)} %constant.97.clone.1), kind=kCustom, calls=%fused_computation.7 | custom fusion | flops 131072 | bytes 139776 | tf_op jit(solution)/shard_map/scatter-add | solution.py:47
  184.1 1.5 slice.540
  185.6 2.2 copy.65
  187.8 0.1 copy.66
  187.8 1.9 collective-permute-start.2
  189.8 3.7 collective-permute-start.3
  193.6 0.7 collective-permute-done.3
  194.2 0.6 fusion.24
  194.9 0.2 stack.5
  195.1 31.7 %all_to_all.5 = f32[16,8,4096]{2,1,0:T(8,128)S(1)} all-to-all(f32[16,8,4096]{2,1,0:T(8,128)S(1)} %stack.5), channel_id=1, replica_groups=mesh['probe'=16,'space'=32] {'probe'}, dimensions={0} | all-to-all | bytes 4194304 | tf_op jit(solution)/shard_map/all_to_all | solution.py:83
  226.8 1.3 copy-done
  228.2 2.4 fusion.2
  230.6 0.2 all-reduce.5.cloned.1.call-start
  230.9 187.5 %all-reduce.3.cloned.1.call-done = f32[128,128]{0,1:T(8,128)} async-done(((f32[128,128]{0,1:T(8,128)}), f32[128,128]{0,1:T(8,128)}) %all-reduce.3.cloned.1.call-update) | async-done | bytes 65552 | tf_op jit(solution)/shard_map/psum | solution.py:51
  418.4 0.9 copy.59
  419.3 0.9 fusion.11
  420.2 11.7 %cholesky.44 = f32[128,128]{1,0:T(8,128)S(1)} custom-call(f32[128,128]{1,0:T(8,128)S(1)} %fusion.11), custom_call_target="Cholesky" | custom-call | tf_op jit(solution)/shard_map/jit(cholesky)/cholesky | solution.py:58
  431.9 0.6 compare_reduce_fusion.1
  432.6 0.7 fusion.15
  433.2 9.8 %custom-call.6 = f32[1,128,128]{1,2,0:T(8,128)S(1)} custom-call(f32[1,128,128]{2,1,0:T(8,128)S(1)} %fusion.15), custom_call_target="InvertDiagBlocksLowerTriangular" | custom-call | tf_op jit(solution)/shard_map/triangular_solve/custom-call.0 | solution.py:59
  443.0 3.5 fusion
  446.5 2.4 fusion.35
  449.0 179.9 %all-reduce.5.cloned.1.call-done = f32[128,128]{0,1:T(8,128)} async-done(((f32[128,128]{0,1:T(8,128)}), f32[128,128]{0,1:T(8,128)}) %all-reduce.5.cloned.1.call-update) | async-done | bytes 65552 | tf_op jit(solution)/shard_map/psum | solution.py:51
  628.9 0.9 copy.61
  629.8 0.9 fusion.9
  630.7 11.9 %cholesky.55 = f32[128,128]{1,0:T(8,128)S(1)} custom-call(f32[128,128]{1,0:T(8,128)S(1)} %fusion.9), custom_call_target="Cholesky" | custom-call | tf_op jit(solution)/shard_map/jit(cholesky)/cholesky | solution.py:63
  642.7 0.7 compare_reduce_fusion
  643.4 2.3 convolution_multiply_fusion
  645.6 0.7 select_bitcast_fusion
  646.3 9.8 %custom-call.7 = f32[1,128,128]{1,2,0:T(8,128)S(1)} custom-call(f32[1,128,128]{2,1,0:T(8,128)S(1)} %select_bitcast_fusion), custom_call_target="InvertDiagBlocksLowerTriangular" | custom-call | tf_op jit(solution)/shard_map/triangular_solve/custom-call.0 | solution.py:64
  656.2 1.9 fusion.7
  658.1 0.7 dynamic-slice_multiply_fusion
  (19 shorter events, 0.3 us)
Async XLA Ops:
  7.2 411.2 %all-reduce.3.cloned.1.call-start = ((), (), s32[]{:S(2)}) async-start(), calls=%async_computation.1 | async-start | bytes 131072 | tf_op jit(solution)/shard_map/psum | solution.py:51
  7.9 19.3 %collective-permute-start = (f32[8,128]{1,0:T(8,128)S(1)}, f32[8,128]{1,0:T(8,128)S(1)}, u32[]{:S(2)}, u32[]{:S(2)}) collective-permute-start(f32[8,128]{1,0:T(8,128)S(1)} %get-tuple-element.103), channel_id=1, source_target_pairs={{0,1},{1,2},{2,3},{3,4},{4,5},{5,6},{6,7},{7,8},{8,9},{9,10},{10,1... | collective-permute-start | bytes 12296 | tf_op jit(solution)/shard_map/ppermute | solution.py:16
  12.8 14.4 %collective-permute-start.1 = (f32[8,128]{1,0:T(8,128)S(1)}, f32[8,128]{1,0:T(8,128)S(1)}, u32[]{:S(2)}, u32[]{:S(2)}) collective-permute-start(f32[8,128]{1,0:T(8,128)S(1)} %get-tuple-element.104), channel_id=1, source_target_pairs={{1,0},{2,1},{3,2},{4,3},{5,4},{6,5},{7,6},{8,7},{9,8},{10,9},{11,1... | collective-permute-start | bytes 12296 | tf_op jit(solution)/shard_map/ppermute | solution.py:19
  185.6 7.9 %copy-start.1 = (f32[8,4096]{1,0:T(8,128)S(1)}, f32[8,4096]{1,0:T(8,128)}, u32[]{:S(2)}) copy-start(f32[8,4096]{1,0:T(8,128)} %param.12) | copy-start | bytes 393220
  185.6 7.9 %copy-start.2 = (f32[4096]{0:T(1024)S(1)}, f32[4096]{0:T(1024)}, u32[]{:S(2)}) copy-start(f32[4096]{0:T(1024)} %param.15) | copy-start | bytes 49156
  187.8 5.7 collective-permute-start.2
  189.8 4.4 collective-permute-start.3
  226.8 1.4 copy-start
  230.6 398.3 %all-reduce.5.cloned.1.call-start = ((), (), s32[]{:S(2)}) async-start(), calls=%async_computation.2 | async-start | bytes 131072 | tf_op jit(solution)/shard_map/psum | solution.py:51
Sparse Core Ops, SparseCore 0:
  230.8 187.5 all-reduce.2
  449.1 179.7 all-reduce.4
